TPU v7x, 128 devices: a whole 4x4x4 slice. The times are simulated.
128 devices in a mesh: fsdp: 8 (over z, core), emb: 16 (over y, x).
Axes of the slice: x: 4, y: 4, z: 4, core: 2. Of those that a mesh axis runs over, the one named last changes fastest.
Arguments:
- item_table: float32 [524288, 256], P(('fsdp', 'emb')), may hold values from -6 to 6
- item_owner: int32 [128, 1024, 1], P(('fsdp', 'emb')), may hold values from 0 to 127; in each aligned block of 1024 rows (0 to 1023, 1024 to 2047, ..., all dimensions but the last counted through in order) at most 16 rows name the same one
- item_row: int32 [128, 1024], P(('fsdp', 'emb')), may hold values from 0 to 4095
- staleness: int32 [524288], P(('fsdp', 'emb')), may hold values from 0 to 3
- w_proj: bfloat16 [2, 256, 1024], P(None, 'fsdp'), may hold values from -0.375 to 0.375
- w_out: bfloat16 [2, 256, 256], P(None, 'fsdp'), may hold values from -0.375 to 0.375
- out_grad: bfloat16 [128, 1024, 256], P(('fsdp', 'emb')), may hold values from -6 to 6
Outputs:
- new_table: float32 [524288, 256], P(('fsdp', 'emb'))
- w_proj_grad: float32 [2, 256, 1024], P(None, 'fsdp')
- w_out_grad: float32 [2, 256, 256], P(None, 'fsdp')
Inputs may be any that keep to these rules, and one draw needn't show every extreme that they name: `item_owner`: in each user's history no owner is named more than 16 times, a bound that some block reaches in every draw.
All inputs are finite; a program needn't handle non-finite values.
Results may differ from a plain program's by a relative error of at most 0.023.
Values may be sent and summed in bfloat16 or wider, within the bound.
A program may use at most 128 MiB of HBM per device.

v0:
```python
import jax
import jax.numpy as jnp
from jax import lax
from jax.sharding import PartitionSpec as P

DH = 64
EPSILON = 1e-05


def normalize(value):
    center = value - jnp.mean(value, axis=-1, keepdims=True)
    inverse = lax.rsqrt(jnp.mean(center * center, axis=-1, keepdims=True) + EPSILON)
    return (center * inverse, inverse)


def norm_back(gradient, normed, inverse):
    return inverse * (
        gradient
        - jnp.mean(gradient, axis=-1, keepdims=True)
        - normed * jnp.mean(gradient * normed, axis=-1, keepdims=True)
    )


def silu_slope(value):
    logistic = jax.nn.sigmoid(value)
    return logistic * (1.0 + value * (1.0 - logistic))


def causal(first_row, block_rows, length):
    query_pos = first_row + lax.broadcasted_iota(jnp.int32, (block_rows, length), 0)
    key_pos = lax.broadcasted_iota(jnp.int32, (block_rows, length), 1)
    return key_pos <= query_pos


def attend(queries, key_rows, values, block_rows, score_scale):
    length = queries.shape[0]
    results = []
    for block_index in range(length // block_rows):
        first_row = block_index * block_rows
        end_row = first_row + block_rows
        query_part = queries[first_row:end_row]
        scores = (
            jnp.einsum(
                "qhd,khd->hqk", query_part, key_rows[:end_row], preferred_element_type=jnp.float32
            )
            * score_scale
        )
        visible = causal(first_row, block_rows, end_row)[None]
        attn = jnp.where(visible, jax.nn.silu(scores), 0.0).astype(jnp.bfloat16)
        results.append(
            jnp.einsum("hqk,khd->qhd", attn, values[:end_row], preferred_element_type=jnp.float32)
        )
    mixture = jnp.concatenate(results, axis=0)
    return mixture.reshape(length, -1)


def attend_back(queries, key_rows, values, grad_mix, block_rows, score_scale):
    length = queries.shape[0]
    grad_keys = jnp.zeros(queries.shape, jnp.float32)
    grad_values = jnp.zeros(queries.shape, jnp.float32)
    query_grads = []
    for block_index in range(length // block_rows):
        first_row = block_index * block_rows
        end_row = first_row + block_rows
        query_part = queries[first_row:end_row]
        grad_part = grad_mix[first_row:end_row]
        key_part = key_rows[:end_row]
        value_part = values[:end_row]
        scores = (
            jnp.einsum("qhd,khd->hqk", query_part, key_part, preferred_element_type=jnp.float32)
            * score_scale
        )
        visible = causal(first_row, block_rows, end_row)[None]
        attn = jnp.where(visible, jax.nn.silu(scores), 0.0).astype(jnp.bfloat16)
        grad_attn = jnp.einsum(
            "qhd,khd->hqk", grad_part, value_part, preferred_element_type=jnp.float32
        )
        grad_values = grad_values.at[:end_row].add(
            jnp.einsum("hqk,qhd->khd", attn, grad_part, preferred_element_type=jnp.float32)
        )
        grad_scores = jnp.where(visible, grad_attn * silu_slope(scores), 0.0).astype(jnp.bfloat16)
        query_grads.append(
            jnp.einsum("hqk,khd->qhd", grad_scores, key_part, preferred_element_type=jnp.float32)
            * score_scale
        )
        grad_keys = grad_keys.at[:end_row].add(
            jnp.einsum("hqk,qhd->khd", grad_scores, query_part, preferred_element_type=jnp.float32)
            * score_scale
        )
    grad_queries = jnp.concatenate(query_grads, axis=0)
    return (
        grad_queries.reshape(length, -1),
        grad_keys.reshape(length, -1),
        grad_values.reshape(length, -1),
    )


def layer_parts(hidden, proj_weight, out_weight, block_rows):
    length = hidden.shape[0]
    width = out_weight.shape[0]
    head_count = width // DH
    hidden_float = hidden.astype(jnp.float32)
    normed_float, inverse_hidden = normalize(hidden_float)
    normed = normed_float.astype(jnp.bfloat16)
    pre_act = jnp.dot(normed, proj_weight, preferred_element_type=jnp.float32)
    projected = jax.nn.silu(pre_act).astype(jnp.bfloat16)
    gating = projected[:, :width]
    values = projected[:, width : 2 * width].reshape(length, head_count, DH)
    queries = projected[:, 2 * width : 3 * width].reshape(length, head_count, DH)
    key_rows = projected[:, 3 * width :].reshape(length, head_count, DH)
    mixture = attend(queries, key_rows, values, block_rows, DH ** (-0.5))
    mix_normed, inverse_mix = normalize(mixture)
    gated_out = (mix_normed * gating.astype(jnp.float32)).astype(jnp.bfloat16)
    return dict(
        hidden_float=hidden_float,
        normed_float=normed_float,
        inverse_hidden=inverse_hidden,
        normed=normed,
        pre_act=pre_act,
        gating=gating,
        values=values,
        queries=queries,
        key_rows=key_rows,
        mix_normed=mix_normed,
        inverse_mix=inverse_mix,
        gated_out=gated_out,
    )


def layer_forward(hidden, proj_weight, out_weight, block_rows):
    parts = layer_parts(hidden, proj_weight, out_weight, block_rows)
    branch = jnp.dot(parts["gated_out"], out_weight, preferred_element_type=jnp.float32)
    return ((parts["hidden_float"] + branch).astype(jnp.bfloat16), parts)


def layer_backward(hidden, grad_out, proj_weight, out_weight, block_rows, parts):
    if parts is None:
        parts = layer_parts(hidden, proj_weight, out_weight, block_rows)
    length = hidden.shape[0]
    width = out_weight.shape[0]
    grad_round = grad_out.astype(jnp.bfloat16)
    gw_out = jnp.dot(parts["gated_out"].T, grad_round, preferred_element_type=jnp.float32)
    grad_gated = jnp.dot(grad_round, out_weight.T, preferred_element_type=jnp.float32)
    grad_gate = grad_gated * parts["mix_normed"]
    grad_mixture = norm_back(
        grad_gated * parts["gating"].astype(jnp.float32), parts["mix_normed"], parts["inverse_mix"]
    )
    grad_mix = grad_mixture.astype(jnp.bfloat16).reshape(length, width // DH, DH)
    grad_queries, grad_keys, grad_values = attend_back(
        parts["queries"], parts["key_rows"], parts["values"], grad_mix, block_rows, DH ** (-0.5)
    )
    grad_proj = jnp.concatenate([grad_gate, grad_values, grad_queries, grad_keys], axis=1)
    grad_pre = (grad_proj * silu_slope(parts["pre_act"])).astype(jnp.bfloat16)
    gw_proj = jnp.dot(parts["normed"].T, grad_pre, preferred_element_type=jnp.float32)
    grad_normed = jnp.dot(grad_pre, proj_weight.T, preferred_element_type=jnp.float32)
    grad_in = grad_out + norm_back(grad_normed, parts["normed_float"], parts["inverse_hidden"])
    return (grad_in, gw_proj, gw_out)


def ask_owners(payload):
    return lax.all_to_all(payload, ("fsdp", "emb"), split_axis=0, concat_axis=0, tiled=True)


def return_rows(payload):
    return lax.all_to_all(payload, ("fsdp", "emb"), split_axis=0, concat_axis=0, tiled=True)


def send_gradients(payload):
    return lax.all_to_all(
        payload.astype(jnp.bfloat16), ("fsdp", "emb"), split_axis=0, concat_axis=0, tiled=True
    ).astype(payload.dtype)


def local(item_table, item_owner, item_row, staleness, w_proj, w_out, out_grad):
    fsdp_count = lax.axis_size("fsdp")
    emb_count = lax.axis_size("emb")
    owners = fsdp_count * emb_count
    length = item_row.shape[1]
    capacity = 2 * length // owners
    table_rows = item_table.shape[0]
    width = item_table.shape[1]
    owner_of = item_owner[0, :, 0]
    offset = item_row[0]
    member = (owner_of[:, None] == jnp.arange(owners, dtype=jnp.int32)[None, :]).astype(jnp.int32)
    earlier = jnp.cumsum(member, axis=0) - member
    slot_index = jnp.sum(earlier * member, axis=1)
    target = owner_of * capacity + slot_index
    request = (
        jnp.full((owners * capacity,), -1, jnp.int32)
        .at[target]
        .set(offset)
        .reshape(owners, capacity)
    )
    requested = ask_owners(request)
    present = requested >= 0
    safe_rows = jnp.where(present, requested, 0)
    looked_up = jnp.where(present[:, :, None], item_table[safe_rows], 0.0).astype(jnp.bfloat16)
    returned = return_rows(looked_up)
    item_rows = returned.reshape(owners * capacity, width)[target]
    proj_all, out_all = (
        lax.all_gather(w_proj, "fsdp", axis=1, tiled=True),
        lax.all_gather(w_out, "fsdp", axis=1, tiled=True),
    )
    layer_count = w_proj.shape[0]
    block_rows = min(512, length)
    inputs = [item_rows]
    saved_parts = []
    layer_index = 0
    next_hidden, parts = layer_forward(
        inputs[-1], proj_all[layer_index], out_all[layer_index], block_rows
    )
    inputs.append(next_hidden)
    saved_parts.append(parts)
    saved_parts.append(None)
    gradient = out_grad[0].astype(jnp.float32)
    proj_list = []
    out_list = []
    for layer_index in reversed(range(layer_count)):
        gradient, gw_proj, gw_out = layer_backward(
            inputs[layer_index],
            gradient,
            proj_all[layer_index],
            out_all[layer_index],
            block_rows,
            saved_parts[layer_index],
        )
        proj_list.insert(0, gw_proj)
        out_list.insert(0, gw_out)
    proj_grads = jnp.stack(proj_list)
    out_grads = jnp.stack(out_list)
    outgoing = jnp.zeros((owners * capacity, width), jnp.float32).at[target].set(gradient)
    incoming = send_gradients(outgoing.reshape(owners, capacity, width))
    scatter_at = jnp.where(present, requested, table_rows).reshape(-1)
    table_grad = (
        jnp.zeros((table_rows, width), jnp.float32)
        .at[scatter_at]
        .add(incoming.reshape(-1, width), mode="drop")
    )
    step_rate = 0.5 / (1.0 + staleness.astype(jnp.float32))
    new_table = item_table - step_rate[:, None] * table_grad
    whole_proj, whole_out = (
        lax.psum(proj_grads.astype(jnp.bfloat16), "emb").astype(jnp.float32),
        lax.psum(out_grads.astype(jnp.bfloat16), "emb").astype(jnp.float32),
    )
    summed_proj, summed_out = (
        lax.psum_scatter(
            whole_proj.astype(jnp.bfloat16), "fsdp", scatter_dimension=1, tiled=True
        ).astype(jnp.float32),
        lax.psum_scatter(
            whole_out.astype(jnp.bfloat16), "fsdp", scatter_dimension=1, tiled=True
        ).astype(jnp.float32),
    )
    norm_scale = (owners * length) ** (-0.5)
    return (new_table, summed_proj * norm_scale, summed_out * norm_scale)


def solution(mesh):
    return jax.shard_map(
        local,
        mesh=mesh,
        in_specs=(
            P(("fsdp", "emb"), None),
            P(("fsdp", "emb"), None, None),
            P(("fsdp", "emb"), None),
            P(("fsdp", "emb")),
            P(None, "fsdp", None),
            P(None, "fsdp", None),
            P(("fsdp", "emb"), None, None),
        ),
        out_specs=(P(("fsdp", "emb"), None), P(None, "fsdp", None), P(None, "fsdp", None)),
        check_vma=False,
    )
```

profile of v0, /device:TPU:0, one launch (start us, length us, event | category | flops | bytes accessed | tf_op | source)
XLA Modules:
  0.0 354.0 jit_solution(6492825547903899997)
XLA Ops:
  10.1 4.5 %scatter_custom_fusion = s32[2048]{0:T(1024)S(1)} fusion(s32[1024]{0:T(1024)S(1)} %bitcast.264, s32[1024]{0:T(1024)} %bitcast.268, s32[]{:T(128)} %constant.274.clone.1), kind=kCustom, calls=%fused_computation.161 | custom fusion | bytes 8704 | tf_op jit(solution)/shard_map/scatter | solution.py:191
  15.3 11.1 %all-to-all-start = ((s32[128,1,16]{2,1,0:T(1,128)}), s32[128,1,16]{2,1,0:T(1,128)S(1)}, u32[]{:S(2)}, u32[]{:S(2)}) async-start(s32[128,1,16]{2,1,0:T(1,128)} %bitcast.9), calls=%async_computation | async-start | bytes 131072 | tf_op jit(solution)/shard_map/all_to_all | solution.py:161
  27.2 8.7 %all-to-all-done = s32[128,1,16]{2,1,0:T(1,128)S(1)} async-done(((s32[128,1,16]{2,1,0:T(1,128)}), s32[128,1,16]{2,1,0:T(1,128)S(1)}, u32[]{:S(2)}, u32[]{:S(2)}) %all-to-all-start) | async-done | bytes 8224 | tf_op jit(solution)/shard_map/all_to_all | solution.py:161
  36.2 8.8 %gather_fusion = bf16[2048,256]{1,0:T(8,128)(2,1)S(1)} fusion(f32[4096,256]{1,0:T(8,128)} %param.31, s32[2048]{0:T(1024)S(1)} %broadcast_clamp_fusion), kind=kCustom, calls=%fused_computation | custom fusion | bytes 2105344 | tf_op jit(solution)/shard_map/gather | solution.py:197
  46.3 4.6 %all-to-all-start.1 = ((bf16[128,16,256]{2,1,0:T(8,128)(2,1)}), bf16[128,16,256]{2,1,0:T(8,128)(2,1)S(1)}, u32[]{:S(2)}, u32[]{:S(2)}) async-start(bf16[128,16,256]{2,1,0:T(8,128)(2,1)} %select_convert_fusion.8), calls=%async_computation.1 | async-start | bytes 2097152 | tf_op jit(solution)/shard_map/all_to_all | solution.py:165
  51.2 17.5 %all_gather.7 = bf16[2,256,256]{2,1,0:T(8,128)(2,1)} all-gather(bf16[2,32,256]{2,1,0:T(8,128)(2,1)S(1)} %copy-done.18), channel_id=1, replica_groups=mesh['fsdp'=8,'emb'=16] {'fsdp'}, dimensions={1}, use_global_device_ids=true | all-gather | bytes 294912 | tf_op jit(solution)/shard_map/all_gather | solution.py:202
  70.7 4.1 %gather_fusion.1 = bf16[1024,256]{1,0:T(8,128)(2,1)S(1)} fusion(bf16[2048,256]{1,0:T(8,128)(2,1)S(1)} %bitcast.219, s32[1024]{0:T(1024)S(1)} %broadcast_clamp_fusion.1), kind=kCustom, calls=%fused_computation.1 | custom fusion | bytes 1052672 | tf_op jit(solution)/shard_map/gather | solution.py:199
  75.3 4.3 %multiply_convert_fusion.1 = (bf16[1024,1024]{0,1:T(8,128)(2,1)S(1)}, f32[1024,1024]{0,1:T(8,128)}) fusion(bf16[2,256,1024]{2,1,0:T(8,128)(2,1)} %all-gather.2.cloned.1.call-done, bf16[1024,256]{0,1:T(8,128)(2,1)S(1)} %copy.30, f32[1024]{0:T(1024)S(1)} %add_rsqrt_fusion.3, f32[1024]{0:T(1024)S(1)} %broadcast_multiply_fusion.11), kind=kOutput, calls=%fused_computation.24 | convolution fusion | flops 543162368 | bytes 7348224 | tf_op jit(solution)/shard_map/dot_general | solution.py:105
  80.7 5.5 %select_convert_fusion.3 = (bf16[4,512,1024]{2,1,0:T(8,128)(2,1)S(1)}, f32[4,512,1024]{2,1,0:T(8,128)}) fusion(pred[512,1024]{1,0:T(8,128)(4,1)S(1)} %copy-done.13, bf16[512,4,64]{0,2,1:T(8,128)(2,1)S(1)} %bitcast.240, bf16[1024,4,64]{0,2,1:T(8,128)(2,1)S(1)} %bitcast.228), kind=kOutput, calls=%fused_computation.9 | convolution fusion | flops 283115520 | bytes 13893632 | tf_op jit(solution)/shard_map/qhd,khd->hqk/dot_general | solution.py:43
  87.6 3.5 select_convert_fusion.7
  94.7 5.7 %select_convert_fusion.2 = (bf16[4,512,1024]{2,1,0:T(8,128)(2,1)S(1)}, f32[4,512,1024]{2,1,0:T(8,128)}) fusion(pred[512,1024]{1,0:T(8,128)(4,1)S(1)} %copy-done.13, bf16[512,4,64]{0,2,1:T(8,128)(2,1)S(1)} %bitcast.242, bf16[1024,4,64]{0,2,1:T(8,128)(2,1)S(1)} %bitcast.232), kind=kOutput, calls=%fused_computation.7 | convolution fusion | flops 283115520 | bytes 13893632 | tf_op jit(solution)/shard_map/qhd,khd->hqk/dot_general | solution.py:43
  100.4 1.4 convolution_bitcast_fusion.6
  101.8 1.7 select_convert_fusion.6
  105.5 2.2 select_convert_fusion.5
  109.4 6.5 %select_convert_fusion.1 = bf16[4,512,1024]{2,1,0:T(8,128)(2,1)S(1)} fusion(f32[4,512,1024]{2,1,0:T(8,128)} %get-tuple-element.174, pred[512,1024]{1,0:T(8,128)(4,1)S(1)} %copy-done.14, bf16[512,4,64]{0,2,1:T(8,128)(2,1)S(1)} %bitcast.238, bf16[1024,4,64]{0,2,1:T(8,128)(2,1)S(1)} %bitcast.235), kind=kOutput, calls=%fused_computation.6 | convolution fusion | flops 291504128 | bytes 13893632 | tf_op jit(solution)/shard_map/qhd,khd->hqk/dot_general | solution.py:75
  115.9 1.4 fusion.24
  119.1 2.0 fusion
  125.0 2.1 select_convert_fusion.4
  127.7 1.5 fusion.27
  130.1 6.5 %select_convert_fusion = bf16[4,512,1024]{2,1,0:T(8,128)(2,1)S(1)} fusion(f32[4,512,1024]{2,1,0:T(8,128)} %get-tuple-element.166, pred[512,1024]{1,0:T(8,128)(4,1)S(1)} %copy-done.15, bf16[512,4,64]{0,2,1:T(8,128)(2,1)S(1)} %bitcast.236, bf16[1024,4,64]{0,2,1:T(8,128)(2,1)S(1)} %bitcast.231), kind=kOutput, calls=%fused_computation.5 | convolution fusion | flops 291504128 | bytes 13893632 | tf_op jit(solution)/shard_map/qhd,khd->hqk/dot_general | solution.py:75
  136.6 2.2 fusion.25
  139.7 1.8 fusion.6
  143.9 3.9 %fusion.1 = bf16[1024,1024]{0,1:T(8,128)(2,1)S(1)} fusion(f32[1024,256]{0,1:T(8,128)S(1)} %bitcast.220, f32[1024,256]{0,1:T(8,128)S(1)} %bitcast.224, f32[1024,256]{0,1:T(8,128)} %bitcast.221, f32[1024,256]{0,1:T(8,128)} %get-tuple-element.141, f32[1024,1024]{0,1:T(8,128)} %get-tuple-element.164), kind=kLoop, calls=%fused_computation.14 | loop fusion | flops 12582912 | bytes 10485760 | tf_op jit(solution)/shard_map/convert_element_type | solution.py:153
  151.1 2.5 fusion.75
  154.3 5.3 %scatter_custom_fusion.1 = f32[2048,256]{1,0:T(8,128)S(1)} fusion(s32[1024]{0:T(1024)S(1)} %bitcast.266, f32[1024,256]{1,0:T(8,128)S(1)} %copy.31, f32[]{:T(128)} %constant.273.clone.1), kind=kCustom, calls=%fused_computation.115 | custom fusion | bytes 2097156 | tf_op jit(solution)/shard_map/scatter | solution.py:231
  160.7 13.4 %all-to-all-start.2 = ((bf16[128,16,256]{2,1,0:T(8,128)(2,1)}), bf16[128,16,256]{2,1,0:T(8,128)(2,1)S(1)}, u32[]{:S(2)}, u32[]{:S(2)}) async-start(bf16[128,16,256]{2,1,0:T(8,128)(2,1)} %bitcast.60), calls=%async_computation.2 | async-start | bytes 2097152 | tf_op jit(solution)/shard_map/all_to_all | solution.py:169
  175.6 2.6 reduce-scatter.5.cloned.1.call-done
  178.2 74.5 %psum.17 = bf16[2,32,256]{2,1,0:T(8,128)(2,1)S(1)} all-reduce(bf16[2,32,256]{2,1,0:T(8,128)(2,1)} %reduce-scatter.5.cloned.1.call-done), channel_id=1, replica_groups=mesh['fsdp'=8,'emb'=16] {'emb'}, use_global_device_ids=true, to_apply=%region_24.25 | all-reduce | flops 16384 | bytes 65536 | tf_op jit(solution)/shard_map/psum | solution.py:243
  253.4 13.9 %scatter_custom_fusion.2 = f32[4096,256]{1,0:T(8,128)} fusion(s32[2048]{0:T(1024)S(1)} %bitcast.267, bf16[2048,256]{1,0:T(8,128)(2,1)S(1)} %bitcast.227, f32[]{:T(128)} %constant.273.clone.1), kind=kCustom, calls=%fused_computation.26 | custom fusion | flops 1048576 | bytes 5242884 | tf_op jit(solution)/shard_map/scatter-add | solution.py:237
  267.3 5.1 %multiply_subtract_fusion = f32[4096,256]{1,0:T(8,128)} fusion(f32[4096,256]{1,0:T(8,128)} %param.31, f32[4096,256]{1,0:T(8,128)} %scatter_custom_fusion.2, f32[4096]{0:T(1024)S(1)} %add_divide_fusion.6), kind=kLoop, calls=%fused_computation.15 | loop fusion | flops 2097152 | bytes 12599296 | tf_op jit(solution)/shard_map/sub | solution.py:240
  272.4 73.3 %all-reduce.6.cloned.1.call-done = bf16[2,32,1024]{2,1,0:T(8,128)(2,1)} async-done(((bf16[2,32,1024]{2,1,0:T(8,128)(2,1)}), bf16[2,32,1024]{2,1,0:T(8,128)(2,1)}) %all-reduce.6.cloned.1.call-update) | async-done | bytes 131088 | tf_op jit(solution)/shard_map/psum | solution.py:242
  345.7 1.6 convert_multiply_fusion.4
  (146 shorter events, 35.3 us)
Async XLA Ops:
  15.3 20.6 %all-to-all-start = ((s32[128,1,16]{2,1,0:T(1,128)}), s32[128,1,16]{2,1,0:T(1,128)S(1)}, u32[]{:S(2)}, u32[]{:S(2)}) async-start(s32[128,1,16]{2,1,0:T(1,128)} %bitcast.9), calls=%async_computation | async-start | bytes 131072 | tf_op jit(solution)/shard_map/all_to_all | solution.py:161
  26.5 48.9 %all-gather.2.cloned.1.call-start = ((), (), s32[]{:S(2)}) async-start(), calls=%async_computation.5 | async-start | bytes 1179648 | tf_op jit(solution)/shard_map/all_gather | solution.py:201
  45.0 5.9 %copy-start = (bf16[1,1024,256]{2,1,0:T(8,128)(2,1)S(1)}, bf16[1,1024,256]{2,1,0:T(8,128)(2,1)}, u32[]{:S(2)}) copy-start(bf16[1,1024,256]{2,1,0:T(8,128)(2,1)} %param.37) | copy-start | bytes 1572868
  45.0 6.2 %copy-start.18 = (bf16[2,32,256]{2,1,0:T(8,128)(2,1)S(1)}, bf16[2,32,256]{2,1,0:T(8,128)(2,1)}, u32[]{:S(2)}) copy-start(bf16[2,32,256]{2,1,0:T(8,128)(2,1)} %param.36) | copy-start | bytes 98308
  46.3 24.4 %all-to-all-start.1 = ((bf16[128,16,256]{2,1,0:T(8,128)(2,1)}), bf16[128,16,256]{2,1,0:T(8,128)(2,1)S(1)}, u32[]{:S(2)}, u32[]{:S(2)}) async-start(bf16[128,16,256]{2,1,0:T(8,128)(2,1)} %select_convert_fusion.8), calls=%async_computation.1 | async-start | bytes 2097152 | tf_op jit(solution)/shard_map/all_to_all | solution.py:165
  50.9 127.3 %reduce-scatter.5.cloned.1.call-start = ((), (), s32[]{:S(2)}) async-start(), calls=%async_computation.8 | async-start | bytes 294912 | tf_op jit(solution)/shard_map/reduce_scatter | solution.py:249
  79.7 1.0 copy-start.13
  79.8 7.7 %copy-start.7 = (bf16[512,256]{0,1:T(8,128)(2,1)}, bf16[512,256]{0,1:T(8,128)(2,1)S(1)}, u32[]{:S(2)}) copy-start(bf16[512,256]{0,1:T(8,128)(2,1)S(1)} %get-tuple-element.149) | copy-start | bytes 786436
  79.9 7.7 %copy-start.9 = (bf16[512,256]{0,1:T(8,128)(2,1)}, bf16[512,256]{0,1:T(8,128)(2,1)S(1)}, u32[]{:S(2)}) copy-start(bf16[512,256]{0,1:T(8,128)(2,1)S(1)} %get-tuple-element.151) | copy-start | bytes 786436
  79.9 11.3 %copy-start.11 = (bf16[512,256]{0,1:T(8,128)(2,1)}, bf16[512,256]{0,1:T(8,128)(2,1)S(1)}, u32[]{:S(2)}) copy-start(bf16[512,256]{0,1:T(8,128)(2,1)S(1)} %get-tuple-element.152) | copy-start | bytes 786436
  86.2 1.4 copy-start.16
  91.1 1.3 copy-start.6
  91.9 1.3 copy-start.20
  92.8 29.1 %copy-start.1 = (bf16[1024,256]{0,1:T(8,128)(2,1)}, bf16[1024,256]{0,1:T(8,128)(2,1)S(1)}, u32[]{:S(2)}) copy-start(bf16[1024,256]{0,1:T(8,128)(2,1)S(1)} %get-tuple-element.170) | copy-start | bytes 1572868
  108.1 1.2 copy-start.14
  119.1 2.0 copy-start.21
  121.1 1.6 copy-start.3
  122.3 1.9 copy-start.12
  122.3 1.9 copy-start.17
  122.3 2.7 copy-start.22
  125.0 2.2 copy-start.10
  125.0 2.6 copy-start.8
  127.6 2.4 copy-start.15
  142.6 124.7 %reduce-scatter.3.cloned.1.call-start = ((), (), s32[]{:S(2)}) async-start(), calls=%async_computation.6 | async-start | bytes 1179648 | tf_op jit(solution)/shard_map/reduce_scatter | solution.py:246
  143.9 4.0 %copy-start.2 = (bf16[1024,256]{0,1:T(8,128)(2,1)S(1)}, bf16[1024,256]{0,1:T(8,128)(2,1)}, u32[]{:S(2)}) copy-start(bf16[1024,256]{0,1:T(8,128)(2,1)} %copy-done.1) | copy-start | bytes 1572868
  143.9 4.0 %copy-start.4 = (bf16[1024,1024]{0,1:T(8,128)(2,1)S(1)}, bf16[1024,1024]{0,1:T(8,128)(2,1)}, u32[]{:S(2)}) copy-start(bf16[1024,1024]{0,1:T(8,128)(2,1)} %copy-done.3) | copy-start | bytes 6291460
  147.9 1.3 copy-start.5
  154.3 19.9 %copy-start.19 = (s32[4096]{0:T(1024)S(1)}, s32[4096]{0:T(1024)}, u32[]{:S(2)}) copy-start(s32[4096]{0:T(1024)} %param.34) | copy-start | bytes 49156
  160.7 92.7 %all-to-all-start.2 = ((bf16[128,16,256]{2,1,0:T(8,128)(2,1)}), bf16[128,16,256]{2,1,0:T(8,128)(2,1)S(1)}, u32[]{:S(2)}, u32[]{:S(2)}) async-start(bf16[128,16,256]{2,1,0:T(8,128)(2,1)} %bitcast.60), calls=%async_computation.2 | async-start | bytes 2097152 | tf_op jit(solution)/shard_map/all_to_all | solution.py:169
  174.1 171.6 %all-reduce.6.cloned.1.call-start = ((), (), s32[]{:S(2)}) async-start(), calls=%async_computation.7 | async-start | bytes 262144 | tf_op jit(solution)/shard_map/psum | solution.py:242
Sparse Core Ops, SparseCore 0:
  29.0 24.6 all-gather.1
  142.7 35.4 reduce-scatter.4
  180.7 32.1 reduce-scatter.2
  267.4 78.2 all-reduce.5
where the time goes:
time: 359 us; the launch traced here: 354 us
  blocking collectives  92 us (26%)
  waiting for transfers between devices  85.3 us (24%)
  matrix products  62.6 us (17%)
  other arithmetic  41.1 us (11%)
  starting transfers between devices  29.3 us (8%)
  local copies, waits for them, and re-layouts  28.8 us (8%)
  between operations  14.8 us (4%)
    psum x1, blocking collectives, local(): lax.psum(out_grads.astype(jnp.bfloat16), 'emb').astype(jnp.float32)  74.5 us
    psum x1, waiting for transfers between devices, local(): lax.psum(proj_grads.astype(jnp.bfloat16), 'emb').astype(jnp.float32)  73.3 us
    all_gather x1, blocking collectives, local(): lax.all_gather(w_out, 'fsdp', axis=1, tiled=True)  17.5 us
    dot_general x4, matrix products, attend_back(): jnp.einsum('qhd,khd->hqk', grad_part, value_part, preferred_element_type=...  17.4 us
    dot_general x4, matrix products, attend(): jnp.einsum('qhd,khd->hqk', query_part, key_rows[:end_row], preferred_elem...  16.4 us
    scatter-add x1, other arithmetic, local(): table_grad = jnp.zeros((table_rows, width), jnp.float32).at[scatter_at].a...  13.9 us
    all_to_all x1, starting transfers between devices, send_gradients(): lax.all_to_all(payload.astype(jnp.bfloat16), ('fsdp', 'emb'), split_axis=...  13.4 us
    all_to_all x1, starting transfers between devices, ask_owners(): lax.all_to_all(payload, ('fsdp', 'emb'), split_axis=0, concat_axis=0, til...  11.1 us
  transfers between devices with their start and end apart: 7, of which 3 were waited for; matrix products, arithmetic and copies ran while one was open for 16% of the time, Pallas kernels for 0%

commit v1 on v0

--- a/solution.py
+++ b/solution.py
@@ -240,7 +240,7 @@
     new_table = item_table - step_rate[:, None] * table_grad
     whole_proj, whole_out = (
         lax.psum(proj_grads.astype(jnp.bfloat16), "emb").astype(jnp.float32),
-        lax.psum(out_grads.astype(jnp.bfloat16), "emb").astype(jnp.float32),
+        jnp.sum(lax.all_gather(out_grads.astype(jnp.bfloat16), "emb"), axis=0).astype(jnp.float32),
     )
     summed_proj, summed_out = (
         lax.psum_scatter(

time: 359 us -> 374 us (1.042)
  waiting for transfers between devices: 85.3 us -> 176 us
  blocking collectives: 92 us -> 18.2 us
    psum x1 -> x0, blocking collectives: 74.5 us -> none  [local(): lax.psum(out_grads.astype(jnp.bfloat16), 'emb').astype(jnp.float32)]
    all_gather x0 -> x1, waiting for transfers between devices: none -> 42.3 us  [local(): lax.all_gather(out_grads.astype(jnp.bfloat16), 'emb')]
    reduce_scatter x1, waiting for transfers between devices: 2.63 us -> 30.9 us  [local(): lax.psum_scatter(whole_out.astype(jnp.bfloat16), 'fsdp', scatter_dimensio...]
    reduce_scatter x1, waiting for transfers between devices: 0.01 us -> 16.5 us  [local(): lax.psum_scatter(whole_proj.astype(jnp.bfloat16), 'fsdp', scatter_dimensi...]
  transfers between devices with their start and end apart: 7 -> 8, of which waited for: 3 -> 6; matrix products, arithmetic and copies ran while one was open for 16% -> 15% of each run, Pallas kernels for 0% -> 0%
where the time goes in v1:
time: 374 us; the launch traced here: 369 us
  waiting for transfers between devices  176 us (47%)
  matrix products  62.2 us (17%)
  other arithmetic  41.1 us (11%)
  local copies, waits for them, and re-layouts  29.4 us (8%)
  starting transfers between devices  26.8 us (7%)
  blocking collectives  18.2 us (5%)
  between operations  14.8 us (4%)
    psum x1, waiting for transfers between devices, local(): lax.psum(proj_grads.astype(jnp.bfloat16), 'emb').astype(jnp.float32)  76.1 us
    all_gather x1, waiting for transfers between devices, local(): lax.all_gather(out_grads.astype(jnp.bfloat16), 'emb')  42.3 us
    reduce_scatter x1, waiting for transfers between devices, local(): lax.psum_scatter(whole_out.astype(jnp.bfloat16), 'fsdp', scatter_dimensio...  30.9 us
    all_gather x1, blocking collectives, local(): lax.all_gather(w_out, 'fsdp', axis=1, tiled=True)  18.2 us
    dot_general x4, matrix products, attend_back(): jnp.einsum('qhd,khd->hqk', grad_part, value_part, preferred_element_type=...  17.4 us
    reduce_scatter x1, waiting for transfers between devices, local(): lax.psum_scatter(whole_proj.astype(jnp.bfloat16), 'fsdp', scatter_dimensi...  16.5 us
    dot_general x4, matrix products, attend(): jnp.einsum('qhd,khd->hqk', query_part, key_rows[:end_row], preferred_elem...  16.4 us
    scatter-add x1, other arithmetic, local(): table_grad = jnp.zeros((table_rows, width), jnp.float32).at[scatter_at].a...  13.9 us
  transfers between devices with their start and end apart: 8, of which 6 were waited for; matrix products, arithmetic and copies ran while one was open for 15% of the time, Pallas kernels for 0%

profile of v1, /device:TPU:0, one launch (start us, length us, event | category | flops | bytes accessed | tf_op | source)
XLA Modules:
  0.0 368.6 jit_solution(1693646844928646005)
XLA Ops:
  10.1 4.5 %scatter_custom_fusion = s32[2048]{0:T(1024)S(1)} fusion(s32[1024]{0:T(1024)S(1)} %bitcast.264, s32[1024]{0:T(1024)} %bitcast.268, s32[]{:T(128)} %constant.275.clone.1), kind=kCustom, calls=%fused_computation.161 | custom fusion | bytes 8704 | tf_op jit(solution)/shard_map/scatter | solution.py:191
  15.3 11.1 %all-to-all-start = ((s32[128,1,16]{2,1,0:T(1,128)}), s32[128,1,16]{2,1,0:T(1,128)S(1)}, u32[]{:S(2)}, u32[]{:S(2)}) async-start(s32[128,1,16]{2,1,0:T(1,128)} %bitcast.9), calls=%async_computation | async-start | bytes 131072 | tf_op jit(solution)/shard_map/all_to_all | solution.py:161
  27.2 8.7 %all-to-all-done = s32[128,1,16]{2,1,0:T(1,128)S(1)} async-done(((s32[128,1,16]{2,1,0:T(1,128)}), s32[128,1,16]{2,1,0:T(1,128)S(1)}, u32[]{:S(2)}, u32[]{:S(2)}) %all-to-all-start) | async-done | bytes 8224 | tf_op jit(solution)/shard_map/all_to_all | solution.py:161
  36.2 8.8 %gather_fusion = bf16[2048,256]{1,0:T(8,128)(2,1)S(1)} fusion(f32[4096,256]{1,0:T(8,128)} %param.31, s32[2048]{0:T(1024)S(1)} %broadcast_clamp_fusion), kind=kCustom, calls=%fused_computation | custom fusion | bytes 2105344 | tf_op jit(solution)/shard_map/gather | solution.py:197
  46.3 4.6 %all-to-all-start.1 = ((bf16[128,16,256]{2,1,0:T(8,128)(2,1)}), bf16[128,16,256]{2,1,0:T(8,128)(2,1)S(1)}, u32[]{:S(2)}, u32[]{:S(2)}) async-start(bf16[128,16,256]{2,1,0:T(8,128)(2,1)} %select_convert_fusion.8), calls=%async_computation.1 | async-start | bytes 2097152 | tf_op jit(solution)/shard_map/all_to_all | solution.py:165
  52.0 18.2 %all_gather.11 = bf16[2,256,256]{2,1,0:T(8,128)(2,1)S(1)} all-gather(bf16[2,32,256]{2,1,0:T(8,128)(2,1)S(1)} %copy-done.23), channel_id=1, replica_groups=mesh['fsdp'=8,'emb'=16] {'fsdp'}, dimensions={1}, use_global_device_ids=true | all-gather | bytes 294912 | tf_op jit(solution)/shard_map/all_gather | solution.py:202
  71.4 4.1 %gather_fusion.1 = bf16[1024,256]{1,0:T(8,128)(2,1)S(1)} fusion(bf16[2048,256]{1,0:T(8,128)(2,1)S(1)} %bitcast.219, s32[1024]{0:T(1024)S(1)} %broadcast_clamp_fusion.1), kind=kCustom, calls=%fused_computation.1 | custom fusion | bytes 1052672 | tf_op jit(solution)/shard_map/gather | solution.py:199
  76.0 2.4 multiply_convert_fusion.1
  78.7 5.5 %select_convert_fusion.3 = (bf16[4,512,1024]{2,1,0:T(8,128)(2,1)S(1)}, f32[4,512,1024]{2,1,0:T(8,128)}) fusion(pred[512,1024]{1,0:T(8,128)(4,1)S(1)} %iota_compare_fusion, bf16[512,4,64]{0,2,1:T(8,128)(2,1)S(1)} %bitcast.240, bf16[1024,4,64]{0,2,1:T(8,128)(2,1)S(1)} %bitcast.228), kind=kOutput, calls=%fused_computation.9 | convolution fusion | flops 283115520 | bytes 13893632 | tf_op jit(solution)/shard_map/qhd,khd->hqk/dot_general | solution.py:43
  85.6 3.6 select_convert_fusion.7
  92.8 5.6 %select_convert_fusion.2 = (bf16[4,512,1024]{2,1,0:T(8,128)(2,1)S(1)}, f32[4,512,1024]{2,1,0:T(8,128)}) fusion(pred[512,1024]{1,0:T(8,128)(4,1)S(1)} %iota_compare_fusion, bf16[512,4,64]{0,2,1:T(8,128)(2,1)S(1)} %bitcast.242, bf16[1024,4,64]{0,2,1:T(8,128)(2,1)S(1)} %bitcast.232), kind=kOutput, calls=%fused_computation.7 | convolution fusion | flops 283115520 | bytes 13893632 | tf_op jit(solution)/shard_map/qhd,khd->hqk/dot_general | solution.py:43
  99.8 1.7 select_convert_fusion.6
  103.5 2.1 select_convert_fusion.5
  106.9 1.6 fusion.29
  109.8 6.5 %select_convert_fusion.1 = bf16[4,512,1024]{2,1,0:T(8,128)(2,1)S(1)} fusion(f32[4,512,1024]{2,1,0:T(8,128)} %get-tuple-element.174, pred[512,1024]{1,0:T(8,128)(4,1)} %copy-done.19, bf16[512,4,64]{0,2,1:T(8,128)(2,1)S(1)} %bitcast.238, bf16[1024,4,64]{0,2,1:T(8,128)(2,1)S(1)} %bitcast.235), kind=kOutput, calls=%fused_computation.6 | convolution fusion | flops 291504128 | bytes 13893632 | tf_op jit(solution)/shard_map/qhd,khd->hqk/dot_general | solution.py:75
  116.3 1.4 fusion.24
  119.9 2.0 fusion
  125.6 2.2 select_convert_fusion.4
  130.3 6.5 %select_convert_fusion = bf16[4,512,1024]{2,1,0:T(8,128)(2,1)S(1)} fusion(f32[4,512,1024]{2,1,0:T(8,128)} %get-tuple-element.166, pred[512,1024]{1,0:T(8,128)(4,1)S(1)} %copy-done.20, bf16[512,4,64]{0,2,1:T(8,128)(2,1)S(1)} %bitcast.236, bf16[1024,4,64]{0,2,1:T(8,128)(2,1)S(1)} %bitcast.231), kind=kOutput, calls=%fused_computation.5 | convolution fusion | flops 291504128 | bytes 13893632 | tf_op jit(solution)/shard_map/qhd,khd->hqk/dot_general | solution.py:75
  140.1 2.6 fusion.1
  142.7 2.3 fusion.22
  147.6 2.5 fusion.75
  150.8 5.3 %scatter_custom_fusion.1 = f32[2048,256]{1,0:T(8,128)S(1)} fusion(s32[1024]{0:T(1024)S(1)} %bitcast.266, f32[1024,256]{1,0:T(8,128)S(1)} %copy.31, f32[]{:T(128)} %constant.274.clone.1), kind=kCustom, calls=%fused_computation.115 | custom fusion | bytes 2097156 | tf_op jit(solution)/shard_map/scatter | solution.py:231
  157.2 10.8 %all-to-all-start.2 = ((bf16[128,16,256]{2,1,0:T(8,128)(2,1)}), bf16[128,16,256]{2,1,0:T(8,128)(2,1)S(1)}, u32[]{:S(2)}, u32[]{:S(2)}) async-start(bf16[128,16,256]{2,1,0:T(8,128)(2,1)} %bitcast.60), calls=%async_computation.2 | async-start | bytes 2097152 | tf_op jit(solution)/shard_map/all_to_all | solution.py:169
  169.5 16.5 %reduce-scatter.5.cloned.1.call-done = bf16[2,32,1024]{2,1,0:T(8,128)(2,1)} async-done(((bf16[2,256,1024]{2,1,0:T(8,128)(2,1)}), bf16[2,32,1024]{2,1,0:T(8,128)(2,1)}) %reduce-scatter.5.cloned.1.call-update) | async-done | bytes 131088 | tf_op jit(solution)/shard_map/reduce_scatter | solution.py:246
  187.1 13.9 %scatter_custom_fusion.2 = f32[4096,256]{1,0:T(8,128)} fusion(s32[2048]{0:T(1024)S(1)} %bitcast.267, bf16[2048,256]{1,0:T(8,128)(2,1)S(1)} %bitcast.227, f32[]{:T(128)} %constant.274.clone.1), kind=kCustom, calls=%fused_computation.26 | custom fusion | flops 1048576 | bytes 5242884 | tf_op jit(solution)/shard_map/scatter-add | solution.py:237
  200.9 42.3 %all-gather.5.cloned.1.call-done = bf16[16,2,256,256]{3,2,1,0:T(8,128)(2,1)} async-done(((bf16[1,2,256,256]{3,2,1,0:T(8,128)(2,1)}), bf16[16,2,256,256]{3,2,1,0:T(8,128)(2,1)}) %all-gather.5.cloned.1.call-update) | async-done | bytes 4194320 | tf_op jit(solution)/shard_map/all_gather | solution.py:243
  243.2 3.5 reduce_sum.185
  246.7 5.1 %multiply_subtract_fusion = f32[4096,256]{1,0:T(8,128)} fusion(f32[4096,256]{1,0:T(8,128)} %param.31, f32[4096,256]{1,0:T(8,128)} %scatter_custom_fusion.2, f32[4096]{0:T(1024)S(1)} %add_divide_fusion.6), kind=kLoop, calls=%fused_computation.15 | loop fusion | flops 2097152 | bytes 12599296 | tf_op jit(solution)/shard_map/sub | solution.py:240
  251.9 76.1 %all-reduce.6.cloned.1.call-done = bf16[2,32,1024]{2,1,0:T(8,128)(2,1)} async-done(((bf16[2,32,1024]{2,1,0:T(8,128)(2,1)}), bf16[2,32,1024]{2,1,0:T(8,128)(2,1)}) %all-reduce.6.cloned.1.call-update) | async-done | bytes 131088 | tf_op jit(solution)/shard_map/psum | solution.py:242
  328.0 1.6 convert_multiply_fusion.4
  329.6 30.9 %reduce-scatter.3.cloned.1.call-done = bf16[2,32,256]{2,1,0:T(8,128)(2,1)} async-done(((bf16[2,256,256]{2,1,0:T(8,128)(2,1)}), bf16[2,32,256]{2,1,0:T(8,128)(2,1)}) %reduce-scatter.3.cloned.1.call-update) | async-done | bytes 32784 | tf_op jit(solution)/shard_map/reduce_scatter | solution.py:249
  (159 shorter events, 39.0 us)
Async XLA Ops:
  15.3 20.6 %all-to-all-start = ((s32[128,1,16]{2,1,0:T(1,128)}), s32[128,1,16]{2,1,0:T(1,128)S(1)}, u32[]{:S(2)}, u32[]{:S(2)}) async-start(s32[128,1,16]{2,1,0:T(1,128)} %bitcast.9), calls=%async_computation | async-start | bytes 131072 | tf_op jit(solution)/shard_map/all_to_all | solution.py:161
  26.5 49.6 %all-gather.3.cloned.1.call-start = ((), (), s32[]{:S(2)}) async-start(), calls=%async_computation.5 | async-start | bytes 1179648 | tf_op jit(solution)/shard_map/all_gather | solution.py:201
  45.0 5.9 %copy-start = (bf16[1,1024,256]{2,1,0:T(8,128)(2,1)S(1)}, bf16[1,1024,256]{2,1,0:T(8,128)(2,1)}, u32[]{:S(2)}) copy-start(bf16[1,1024,256]{2,1,0:T(8,128)(2,1)} %param.37) | copy-start | bytes 1572868
  45.0 6.9 %copy-start.23 = (bf16[2,32,256]{2,1,0:T(8,128)(2,1)S(1)}, bf16[2,32,256]{2,1,0:T(8,128)(2,1)}, u32[]{:S(2)}) copy-start(bf16[2,32,256]{2,1,0:T(8,128)(2,1)} %param.36) | copy-start | bytes 98308
  46.3 25.1 %all-to-all-start.1 = ((bf16[128,16,256]{2,1,0:T(8,128)(2,1)}), bf16[128,16,256]{2,1,0:T(8,128)(2,1)S(1)}, u32[]{:S(2)}, u32[]{:S(2)}) async-start(bf16[128,16,256]{2,1,0:T(8,128)(2,1)} %select_convert_fusion.8), calls=%async_computation.1 | async-start | bytes 2097152 | tf_op jit(solution)/shard_map/all_to_all | solution.py:165
  50.9 135.1 %reduce-scatter.5.cloned.1.call-start = ((), (), s32[]{:S(2)}) async-start(), calls=%async_computation.8 | async-start | bytes 1179648 | tf_op jit(solution)/shard_map/reduce_scatter | solution.py:246
  70.2 32.4 %copy-start.11 = (bf16[2,256,256]{2,1,0:T(8,128)(2,1)}, bf16[2,256,256]{2,1,0:T(8,128)(2,1)S(1)}, u32[]{:S(2)}) copy-start(bf16[2,256,256]{2,1,0:T(8,128)(2,1)S(1)} %all_gather.11) | copy-start | bytes 786436
  71.4 21.4 %copy-start.19 = (pred[512,1024]{1,0:T(8,128)(4,1)}, pred[512,1024]{1,0:T(8,128)(4,1)S(1)}, u32[]{:S(2)}) copy-start(pred[512,1024]{1,0:T(8,128)(4,1)S(1)} %iota_compare_fusion) | copy-start | bytes 1572868
  78.6 5.6 %copy-start.1 = (bf16[1024,256]{0,1:T(8,128)(2,1)}, bf16[1024,256]{0,1:T(8,128)(2,1)S(1)}, u32[]{:S(2)}) copy-start(bf16[1024,256]{0,1:T(8,128)(2,1)S(1)} %get-tuple-element.154) | copy-start | bytes 1572868
  78.7 5.5 %copy-start.7 = (bf16[512,256]{0,1:T(8,128)(2,1)}, bf16[512,256]{0,1:T(8,128)(2,1)S(1)}, u32[]{:S(2)}) copy-start(bf16[512,256]{0,1:T(8,128)(2,1)S(1)} %get-tuple-element.150) | copy-start | bytes 786436
  78.7 6.9 %copy-start.13 = (bf16[512,256]{0,1:T(8,128)(2,1)}, bf16[512,256]{0,1:T(8,128)(2,1)S(1)}, u32[]{:S(2)}) copy-start(bf16[512,256]{0,1:T(8,128)(2,1)S(1)} %get-tuple-element.149) | copy-start | bytes 786436
  78.7 6.9 %copy-start.15 = (bf16[512,256]{0,1:T(8,128)(2,1)}, bf16[512,256]{0,1:T(8,128)(2,1)S(1)}, u32[]{:S(2)}) copy-start(bf16[512,256]{0,1:T(8,128)(2,1)S(1)} %get-tuple-element.151) | copy-start | bytes 786436
  78.7 10.5 %copy-start.17 = (bf16[512,256]{0,1:T(8,128)(2,1)}, bf16[512,256]{0,1:T(8,128)(2,1)S(1)}, u32[]{:S(2)}) copy-start(bf16[512,256]{0,1:T(8,128)(2,1)S(1)} %get-tuple-element.152) | copy-start | bytes 786436
  84.2 1.4 copy-start.21
  90.0 1.2 copy-start.25
  92.7 5.7 %copy-start.9 = (bf16[512,256]{0,1:T(8,128)(2,1)}, bf16[512,256]{0,1:T(8,128)(2,1)S(1)}, u32[]{:S(2)}) copy-start(bf16[512,256]{0,1:T(8,128)(2,1)S(1)} %get-tuple-element.144) | copy-start | bytes 786436
  116.3 1.4 copy-start.3
  116.3 1.4 copy-start.10
  117.8 1.0 copy-start.4
  119.9 2.0 copy-start.26
  121.9 1.4 copy-start.12
  123.3 2.3 copy-start.27
  125.6 2.2 copy-start.16
  125.6 2.6 copy-start.14
  128.3 2.0 copy-start.2
  128.3 2.0 copy-start.20
  136.9 1.4 copy-start.8
  146.1 97.0 %all-gather.5.cloned.1.call-start = ((), (), s32[]{:S(2)}) async-start(), calls=%async_computation.6 | async-start | bytes 4456448 | tf_op jit(solution)/shard_map/all_gather | solution.py:243
  150.8 17.3 %copy-start.24 = (s32[4096]{0:T(1024)S(1)}, s32[4096]{0:T(1024)}, u32[]{:S(2)}) copy-start(s32[4096]{0:T(1024)} %param.34) | copy-start | bytes 49156
  157.2 29.9 %all-to-all-start.2 = ((bf16[128,16,256]{2,1,0:T(8,128)(2,1)}), bf16[128,16,256]{2,1,0:T(8,128)(2,1)S(1)}, u32[]{:S(2)}, u32[]{:S(2)}) async-start(bf16[128,16,256]{2,1,0:T(8,128)(2,1)} %bitcast.60), calls=%async_computation.2 | async-start | bytes 2097152 | tf_op jit(solution)/shard_map/all_to_all | solution.py:169
  168.0 160.0 %all-reduce.6.cloned.1.call-start = ((), (), s32[]{:S(2)}) async-start(), calls=%async_computation.9 | async-start | bytes 262144 | tf_op jit(solution)/shard_map/psum | solution.py:242
  186.1 174.4 %reduce-scatter.3.cloned.1.call-start = ((), (), s32[]{:S(2)}) async-start(), calls=%async_computation.7 | async-start | bytes 294912 | tf_op jit(solution)/shard_map/reduce_scatter | solution.py:249
  (4 other events, 4.1 us)
Sparse Core Ops, SparseCore 0:
  29.0 24.6 all-gather.2
  146.3 39.7 reduce-scatter.4
  188.7 54.3 all-gather.4
  246.2 81.7 all-reduce.5
  330.3 30.1 reduce-scatter.2
